TPU v7x, 256 devices: a whole 4x4x8 slice. The times are simulated.
256 devices in a mesh: dp: 8 (over x_hi, y), fsdp: 16 (over z, core), tensor: 2 (over x_lo).
Axes of the slice: x: 4 (x_hi: 2, x_lo: 2; x = x_hi * 2 + x_lo), y: 4, z: 8, core: 2. Of those that a mesh axis runs over, the one named last changes fastest.
Arguments:
- attn_out: bfloat16 [16384, 2560], P(('dp', 'fsdp')), may hold values from -6 to 6
- cotangent: bfloat16 [16384, 5120], P(('dp', 'fsdp'), 'tensor'), may hold values from -6 to 6
- old_weights: bfloat16 [3, 2048, 4096], P(None, 'tensor', 'fsdp'), may hold values from -0.125 to 0.125
- depth_coef: float32 [2], replicated, may hold values from 0.3 to 1
- depth_pick: int32 [2], replicated, may hold values from 0 to 2
- in_blocks: bfloat16 [20, 2, 128, 128], replicated, may hold values from -0.3125 to 0.3125
- in_cols: int32 [20, 2], replicated, may hold values from 0 to 15, all different within a row
- out_blocks: bfloat16 [40, 2, 128, 128], P('tensor'), may hold values from -0.375 to 0.375
- out_cols: int32 [40, 2], P('tensor'), may hold values from 0 to 31, all different within a row
Outputs:
- grown_out: bfloat16 [16384, 5120], P(('dp', 'fsdp'), 'tensor')
- grad_attn: bfloat16 [16384, 2560], P(('dp', 'fsdp'), 'tensor')
- grad_in_blocks: float32 [20, 2, 128, 128], P('tensor')
- grad_out_blocks: float32 [40, 2, 128, 128], P('tensor')
Inputs may be any that keep to these rules, and one draw needn't show every extreme that they name: `in_cols`: each row names 2 different old head blocks; every old head block is named by some row. `out_cols`: each row names 2 different old width blocks; every old width block is named by some row.
All inputs are finite; a program needn't handle non-finite values.
Results may differ from a plain program's by a relative error of at most 0.0095.
Values may be sent and summed in bfloat16 or wider, within the bound.
No kernel may reach another device: no remote copies, remote signals or barrier semaphores. Data moves between devices by JAX's collectives and lax.ppermute only.
A program may use at most 64 MiB of HBM per device.

v0:
```python
import jax
import jax.numpy as jnp
from jax import lax
from jax.sharding import PartitionSpec as P

HEAD = 128
D_OLD = 4096
HG_OLD = 16
HG_NEW = 20
DEPTH_K = 2
BO_OLD = 32


def gathered_mix(mixed_weight):
    return lax.all_gather(mixed_weight, "fsdp", axis=1, tiled=True)


def local(
    attn_out,
    cotangent,
    old_weights,
    depth_coef,
    depth_pick,
    in_blocks,
    in_cols,
    out_blocks,
    out_cols,
):
    highest = lax.Precision.HIGHEST
    tok_rows = attn_out.shape[0]
    tensor_half = lax.axis_index("tensor")
    tensor_count = lax.axis_size("tensor")
    local_old = old_weights.shape[1]
    local_blocks = local_old // HEAD
    rows_in = HG_NEW // tensor_count
    mixed_weight = jnp.zeros(old_weights.shape[1:], jnp.float32)
    for layer_slot in range(DEPTH_K):
        picked = lax.dynamic_index_in_dim(old_weights, depth_pick[layer_slot], 0, keepdims=False)
        mixed_weight = mixed_weight + depth_coef[layer_slot] * picked.astype(jnp.float32)
    mixed_weight = mixed_weight.astype(jnp.bfloat16)
    attn_blocks = attn_out.reshape(tok_rows, HG_NEW, HEAD)
    products = jnp.einsum(
        "trd,rkde->trke", attn_blocks, in_blocks, preferred_element_type=jnp.float32
    )
    local_cols = tensor_half * local_blocks + jnp.arange(local_blocks, dtype=jnp.int32)
    in_hot = (in_cols[:, :, None] == local_cols[None, None, :]).astype(jnp.float32)
    hidden_local = jnp.einsum("trke,rkc->tce", products, in_hot, precision=highest)
    hidden_local = hidden_local.reshape(tok_rows, local_old).astype(jnp.bfloat16)
    full_mix = gathered_mix(mixed_weight)
    old_part = jnp.dot(hidden_local, full_mix, preferred_element_type=jnp.float32)
    old_out = lax.psum(old_part.astype(jnp.bfloat16), "tensor")
    old_selected = jnp.take(old_out.reshape(tok_rows, BO_OLD, HEAD), out_cols, axis=1)
    grown_out = jnp.einsum(
        "trkd,rkde->tre", old_selected, out_blocks, preferred_element_type=jnp.float32
    )
    grown_out = grown_out.reshape(tok_rows, -1).astype(jnp.bfloat16)
    cot_blocks = cotangent.reshape(tok_rows, out_blocks.shape[0], HEAD)
    backward_terms = jnp.einsum(
        "tre,rkde->trkd", cot_blocks, out_blocks, preferred_element_type=jnp.float32
    )
    out_hot = (out_cols[:, :, None] == jnp.arange(BO_OLD, dtype=jnp.int32)[None, None, :]).astype(
        jnp.float32
    )
    grad_part = jnp.einsum("trkd,rkc->tcd", backward_terms, out_hot, precision=highest).reshape(
        tok_rows, D_OLD
    )
    old_grad = lax.psum(grad_part.astype(jnp.bfloat16), "tensor")
    hidden_grad_local = jnp.einsum(
        "to,fo->tf", old_grad, full_mix, preferred_element_type=jnp.float32
    ).astype(jnp.bfloat16)
    hidden_grad = lax.all_gather(hidden_grad_local, "tensor", axis=1, tiled=True)
    my_in_blocks = lax.dynamic_slice_in_dim(in_blocks, tensor_half * rows_in, rows_in, 0)
    my_in_cols = lax.dynamic_slice_in_dim(in_cols, tensor_half * rows_in, rows_in, 0)
    grad_selected = jnp.take(hidden_grad.reshape(tok_rows, HG_OLD, HEAD), my_in_cols, axis=1)
    grad_attn = jnp.einsum(
        "trke,rkde->trd", grad_selected, my_in_blocks, preferred_element_type=jnp.float32
    )
    grad_attn = grad_attn.reshape(tok_rows, rows_in * HEAD).astype(jnp.bfloat16)
    my_attn = lax.dynamic_slice_in_dim(attn_blocks, tensor_half * rows_in, rows_in, 1)
    in_terms = jnp.einsum(
        "trd,trke->rkde", my_attn, grad_selected, preferred_element_type=jnp.float32
    )
    out_terms = jnp.einsum(
        "trkd,tre->rkde", old_selected, cot_blocks, preferred_element_type=jnp.float32
    )
    in_sum, out_sum = lax.psum((in_terms, out_terms), ("dp", "fsdp"))
    grad_scale = float(tok_rows * lax.axis_size("dp") * lax.axis_size("fsdp")) ** (-0.5)
    return (grown_out, grad_attn, in_sum * grad_scale, out_sum * grad_scale)


def solution(mesh):
    placed = (
        P(("dp", "fsdp"), None),
        P(("dp", "fsdp"), "tensor"),
        P(None, "tensor", "fsdp"),
        P(),
        P(),
        P(),
        P(),
        P("tensor", None, None, None),
        P("tensor", None),
    )
    return jax.shard_map(
        local,
        mesh=mesh,
        in_specs=placed,
        out_specs=(
            P(("dp", "fsdp"), "tensor"),
            P(("dp", "fsdp"), "tensor"),
            P("tensor", None, None, None),
            P("tensor", None, None, None),
        ),
        check_vma=False,
    )
```

profile of v0, /device:TPU:6, one launch (start us, length us, event | category | flops | bytes accessed | tf_op | source)
XLA Modules:
  0.0 1481.5 jit_solution(9573268355496351866)
XLA Ops:
  7.2 0.0 copy-start
  7.2 0.0 all-gather.3.cloned.1.call-start
  7.2 1.3 fusion.55
  11.2 1.3 fusion.54
  13.8 3.5 add_convert_fusion
  17.3 0.0 copy-start.6
  17.3 0.0 all-gather.3.cloned.1.call-update
  17.4 0.0 all-reduce.7.cloned.1.call-start
  17.4 1.5 copy.27
  18.9 0.0 copy-start.1
  18.9 0.0 copy-done.6
  18.9 2.0 fusion.56
  21.0 0.0 copy-done.1
  21.0 0.0 copy-start.7
  21.0 3.6 copy.45
  24.6 0.0 copy-done.7
  24.6 0.3 copy.34
  24.9 0.0 copy-done
  24.9 2.0 fusion.57
  26.9 3.6 copy.51
  30.5 0.0 copy-done.9
  30.5 3.5 bitcast_convert_fusion
  34.0 0.0 copy-start.8
  34.0 1.4 copy.71
  35.5 0.0 copy-done.8
  35.5 3.0 fusion.24
  38.5 46.0 %all-gather.3.cloned.1.call-done = bf16[1,1024,4096]{2,1,0:T(8,128)(2,1)} async-done(((bf16[1,1024,256]{2,1,0:T(8,128)(2,1)}), bf16[1,1024,4096]{2,1,0:T(8,128)(2,1)}) %all-gather.3.cloned.1.call-update) | async-done | bytes 8388624 | tf_op jit(solution)/shard_map/all_gather | solution.py:15
  84.5 4.7 fusion.13
  89.1 1.3 copy.72
  90.4 0.0 all-reduce.7.cloned.1.call-update
  90.4 0.0 all-reduce.5.cloned.1.call-start
  90.5 0.1 compare_and_fusion
  90.6 0.1 copy.35
  90.7 0.1 reshape.66
  90.7 0.1 copy.33
  90.8 0.1 copy.29
  91.0 0.1 reshape.58
  91.1 0.1 copy.26
  91.2 72.4 %all-reduce.7.cloned.1.call-done = (bf16[128,32,128]{2,0,1:T(8,128)(2,1)}, bf16[128,4096]{1,0:T(8,128)(2,1)}) async-done(((bf16[128,32,128]{2,0,1:T(8,128)(2,1)}, bf16[128,4096]{1,0:T(8,128)(2,1)}), (bf16[128,32,128]{2,0,1:T(8,128)(2,1)}, bf16[128,4096]{1,0:T(8,128)(2,1)})) %all-reduce.7.cloned.1.call-update) | async-done | bytes 2097168 | tf_op jit(solution)/shard_map/psum | solution.py:51
  163.5 6.6 fusion.27
  170.2 8.7 all_gather.7
  178.9 0.1 copy_bitcast_fusion.2
  179.0 0.7 gather_fusion.1
  179.7 1.1 copy.37
  180.8 3.1 gather_fusion
  183.9 1.8 copy.30
  185.6 0.0 copy-start.2
  185.6 0.0 copy-start.3
  185.7 2.0 fusion.17
  187.7 0.0 copy-done.2
  187.7 0.0 copy-done.3
  187.7 1.4 convolution_bitcast_fusion
  189.1 0.0 copy-start.4
  189.1 0.0 all-reduce.5.cloned.1.call-update
  189.2 1.1 copy-done.4
  190.2 2.2 fusion.23
  192.4 1.9 copy.42
  194.3 0.6 fusion.16
  194.9 1.1 copy.41
  196.0 1273.8 %all-reduce.5.cloned.1.call-done = (f32[10,2,128,128]{2,3,1,0:T(8,128)}, f32[20,2,128,128]{3,2,1,0:T(8,128)}) async-done(((f32[10,2,128,128]{2,3,1,0:T(8,128)}, f32[20,2,128,128]{3,2,1,0:T(8,128)}), (f32[10,2,128,128]{2,3,1,0:T(8,128)}, f32[20,2,128,128]{3,2,1,0:T(8,128)})) %all-reduce.5.cloned.1.call-update) | async-done | bytes 3932176 | tf_op jit(solution)/shard_map/psum | solution.py:86
  1469.8 3.6 broadcast_multiply_fusion
  1473.4 0.0 copy-done.5
  1473.4 0.1 broadcast_multiply_fusion.1
  1473.5 1.5 copy.43
  (7 shorter events, 0.0 us)
Async XLA Ops:
  7.2 17.8 %copy-start = (bf16[20,2,128,128]{3,2,1,0:T(8,128)(2,1)S(1)}, bf16[20,2,128,128]{3,2,1,0:T(8,128)(2,1)}, u32[]{:S(2)}) copy-start(bf16[20,2,128,128]{3,2,1,0:T(8,128)(2,1)} %param.16) | copy-start | bytes 3932164
  7.2 77.3 %all-gather.3.cloned.1.call-start = ((), (), s32[]{:S(2)}) async-start(), calls=%async_computation | async-start | bytes 8912896 | tf_op jit(solution)/shard_map/all_gather | solution.py:15
  17.3 1.6 copy-start.6
  17.4 146.2 %all-reduce.7.cloned.1.call-start = ((), (), s32[]{:S(2)}) async-start(), calls=%async_computation.2 | async-start | bytes 4194304 | tf_op jit(solution)/shard_map/psum | solution.py:51
  18.9 2.1 copy-start.1
  21.0 3.6 copy-start.7
  26.9 3.6 copy-start.9
  34.0 1.4 copy-start.8
  90.4 1379.4 %all-reduce.5.cloned.1.call-start = ((), (), s32[]{:S(2)}) async-start(), calls=%async_computation.1 | async-start | bytes 7864320 | tf_op jit(solution)/shard_map/psum | solution.py:86
  185.6 2.1 copy-start.2
  185.6 2.1 copy-start.3
  189.1 1.1 copy-start.4
  1469.8 3.6 copy-start.5
Sparse Core Ops, SparseCore 0:
  17.5 66.9 all-gather.2
  90.5 72.9 all-reduce.6
  189.3 1280.4 all-reduce.4
where the time goes:
time: 1480 us
  waiting for transfers between devices  1390 us (94%)
  matrix products  28.2 us (2%)
  local copies, waits for them, and re-layouts  27.2 us (2%)
  between operations  17.8 us (1%)
    psum x1, waiting for transfers between devices, local(): in_sum, out_sum = lax.psum((in_terms, out_terms), ('dp', 'fsdp'))  1270 us
    psum x1, waiting for transfers between devices, local(): old_out = lax.psum(old_part.astype(jnp.bfloat16), 'tensor')  72.4 us
    all_gather x1, waiting for transfers between devices, gathered_mix(): return lax.all_gather(mixed_weight, 'fsdp', axis=1, tiled=True)  46 us
  transfers between devices with their start and end apart: 3, of which 3 were waited for; matrix products, arithmetic and copies ran while one was open for 2% of the time, Pallas kernels for 0%

commit v1 on v0

--- a/solution.py
+++ b/solution.py
@@ -83,7 +83,13 @@
     out_terms = jnp.einsum(
         "trkd,tre->rkde", old_selected, cot_blocks, preferred_element_type=jnp.float32
     )
-    in_sum, out_sum = lax.psum((in_terms, out_terms), ("dp", "fsdp"))
+
+    def masks_get(t0, bus_axis, mesh_dim):
+        for t in (bus_axis, mesh_dim):
+            t0 = lax.psum(t0, axis_name=t)
+        return t0
+
+    in_sum, out_sum = masks_get((in_terms, out_terms), "dp", "fsdp")
     grad_scale = float(tok_rows * lax.axis_size("dp") * lax.axis_size("fsdp")) ** (-0.5)
     return (grown_out, grad_attn, in_sum * grad_scale, out_sum * grad_scale)
 

time: 1480 us -> 438 us (0.30)
  waiting for transfers between devices: 1390 us -> 348 us
    psum x1 -> x2, waiting for transfers between devices: 1270 us -> 229 us  [masks_get(): t0 = lax.psum(t0, axis_name=t)]
  transfers between devices with their start and end apart: 3 -> 4, of which waited for: 3 -> 4; matrix products, arithmetic and copies ran while one was open for 2% -> 6% of each run, Pallas kernels for 0% -> 0%
where the time goes in v1:
time: 438 us; the launch traced here: 437 us
  waiting for transfers between devices  348 us (79%)
  matrix products  28.2 us (6%)
  local copies, waits for them, and re-layouts  27.1 us (6%)
  between operations  17.8 us (4%)
  blocking collectives  8.54 us (2%)
  other arithmetic  7.38 us (2%)
    psum x2, waiting for transfers between devices, masks_get(): t0 = lax.psum(t0, axis_name=t)  229 us
    psum x1, waiting for transfers between devices, local(): old_out = lax.psum(old_part.astype(jnp.bfloat16), 'tensor')  72.7 us
    all_gather x1, waiting for transfers between devices, gathered_mix(): return lax.all_gather(mixed_weight, 'fsdp', axis=1, tiled=True)  46 us
  transfers between devices with their start and end apart: 4, of which 4 were waited for; matrix products, arithmetic and copies ran while one was open for 6% of the time, Pallas kernels for 0%

profile of v1, /device:TPU:6, one launch (start us, length us, event | category | flops | bytes accessed | tf_op | source)
XLA Modules:
  0.0 437.3 jit_solution(12904491024456688300)
XLA Ops:
  7.2 0.0 copy-start
  7.2 0.0 all-gather.3.cloned.1.call-start
  7.2 1.3 fusion.55
  11.2 1.3 fusion.54
  13.8 3.5 add_convert_fusion
  17.3 0.0 all-gather.3.cloned.1.call-update
  17.4 0.0 all-reduce.11.cloned.1.call-start
  17.4 1.5 copy.27
  18.9 0.0 copy-start.1
  18.9 0.0 copy-done.6
  18.9 2.0 fusion.56
  21.0 0.0 copy-done.1
  21.0 3.6 copy.45
  24.6 0.0 copy-done.7
  24.6 0.3 copy.34
  24.9 0.0 copy-done
  24.9 2.0 fusion.57
  26.9 3.6 copy.51
  30.4 0.0 copy-done.9
  30.4 3.5 bitcast_convert_fusion
  34.0 0.0 copy-start.8
  34.0 1.4 copy.71
  35.4 0.0 copy-done.8
  35.4 3.0 fusion.24
  38.4 46.0 %all-gather.3.cloned.1.call-done = bf16[1,1024,4096]{2,1,0:T(8,128)(2,1)} async-done(((bf16[1,1024,256]{2,1,0:T(8,128)(2,1)}), bf16[1,1024,4096]{2,1,0:T(8,128)(2,1)}) %all-gather.3.cloned.1.call-update) | async-done | bytes 8388624 | tf_op jit(solution)/shard_map/all_gather | solution.py:15
  84.4 4.7 %fusion.13 = bf16[16,32,8,128]{3,2,1,0:T(8,128)(2,1)S(1)} fusion(bf16[1,1024,4096]{2,1,0:T(8,128)(2,1)} %all-gather.3.cloned.1.call-done, bf16[16,8,8,128]{3,2,1,0:T(8,128)(2,1)S(1)} %bitcast.126), kind=kOutput, calls=%fused_computation.14 | convolution fusion | flops 1074266112 | bytes 9699328 | tf_op jit(solution)/shard_map/dot_general | solution.py:50
  89.1 1.3 copy.72
  90.4 0.0 all-reduce.11.cloned.1.call-update
  90.4 0.0 all-reduce.9.cloned.1.call-start
  90.4 0.1 compare_and_fusion
  90.5 0.1 copy.35
  90.6 0.1 reshape.66
  90.7 0.1 copy.33
  90.8 0.1 copy.29
  90.9 0.1 reshape.58
  91.0 0.1 copy.26
  91.2 72.7 %all-reduce.11.cloned.1.call-done = (bf16[128,32,128]{2,0,1:T(8,128)(2,1)}, bf16[128,4096]{1,0:T(8,128)(2,1)}) async-done(((bf16[128,32,128]{2,0,1:T(8,128)(2,1)}, bf16[128,4096]{1,0:T(8,128)(2,1)}), (bf16[128,32,128]{2,0,1:T(8,128)(2,1)}, bf16[128,4096]{1,0:T(8,128)(2,1)})) %all-reduce.11.cloned.1.call-update) | async-done | bytes 2097168 | tf_op jit(solution)/shard_map/psum | solution.py:51
  163.9 6.6 %fusion.27 = bf16[128,1024]{1,0:T(8,128)(2,1)S(1)} fusion(bf16[128,4096]{1,0:T(8,128)(2,1)} %get-tuple-element.17, bf16[1,1024,4096]{2,1,0:T(8,128)(2,1)} %all-gather.3.cloned.1.call-done), kind=kOutput, calls=%fused_computation.25 | convolution fusion | flops 1073872896 | bytes 9699328 | tf_op jit(solution)/shard_map/to,fo->tf/dot_general | solution.py:68
  170.5 8.5 %all_gather.7 = bf16[128,2048]{1,0:T(8,128)(2,1)S(1)} all-gather(bf16[128,1024]{1,0:T(8,128)(2,1)S(1)} %fusion.27), channel_id=1, replica_groups=mesh['dp'=8,'fsdp'=16,'tensor'=2] {'tensor'}, dimensions={1}, use_global_device_ids=true | all-gather | bytes 786432 | tf_op jit(solution)/shard_map/all_gather | solution.py:71
  179.1 0.1 copy_bitcast_fusion.2
  179.2 0.7 gather_fusion.1
  179.9 1.1 copy.37
  181.0 3.1 gather_fusion
  184.0 1.8 copy.30
  185.8 0.0 copy-start.2
  185.8 0.0 copy-start.3
  185.8 2.0 fusion.17
  187.9 0.0 copy-done.2
  187.9 0.0 copy-done.3
  187.9 1.4 convolution_bitcast_fusion
  189.3 0.0 all-reduce.9.cloned.1.call-update
  189.3 0.0 all-reduce.7.cloned.1.call-start
  189.4 111.8 %all-reduce.9.cloned.1.call-done = (f32[10,2,128,128]{2,3,1,0:T(8,128)}, f32[20,2,128,128]{3,2,1,0:T(8,128)}) async-done(((f32[10,2,128,128]{2,3,1,0:T(8,128)}, f32[20,2,128,128]{3,2,1,0:T(8,128)}), (f32[10,2,128,128]{2,3,1,0:T(8,128)}, f32[20,2,128,128]{3,2,1,0:T(8,128)})) %all-reduce.9.cloned.1.call-update) | async-done | bytes 3932176 | tf_op jit(solution)/shard_map/psum | solution.py:89
  301.2 0.0 all-reduce.7.cloned.1.call-update
  301.2 1.1 copy-done.4
  302.2 2.2 fusion.23
  304.4 1.9 copy.42
  306.3 0.6 fusion.16
  306.9 1.1 copy.41
  308.0 117.5 %all-reduce.7.cloned.1.call-done = (f32[10,2,128,128]{2,3,1,0:T(8,128)}, f32[20,2,128,128]{3,2,1,0:T(8,128)}) async-done(((f32[10,2,128,128]{2,3,1,0:T(8,128)}, f32[20,2,128,128]{3,2,1,0:T(8,128)}), (f32[10,2,128,128]{2,3,1,0:T(8,128)}, f32[20,2,128,128]{3,2,1,0:T(8,128)})) %all-reduce.7.cloned.1.call-update) | async-done | bytes 3932176 | tf_op jit(solution)/shard_map/psum | solution.py:89
  425.6 3.6 broadcast_multiply_fusion
  429.2 0.0 copy-done.5
  429.2 0.1 broadcast_multiply_fusion.1
  429.3 1.5 copy.43
  (10 shorter events, 0.0 us)
Async XLA Ops:
  7.2 17.7 %copy-start = (bf16[20,2,128,128]{3,2,1,0:T(8,128)(2,1)S(1)}, bf16[20,2,128,128]{3,2,1,0:T(8,128)(2,1)}, u32[]{:S(2)}) copy-start(bf16[20,2,128,128]{3,2,1,0:T(8,128)(2,1)} %param.16) | copy-start | bytes 3932164
  7.2 77.2 %all-gather.3.cloned.1.call-start = ((), (), s32[]{:S(2)}) async-start(), calls=%async_computation | async-start | bytes 8912896 | tf_op jit(solution)/shard_map/all_gather | solution.py:15
  17.3 1.6 copy-start.6
  17.4 146.5 %all-reduce.11.cloned.1.call-start = ((), (), s32[]{:S(2)}) async-start(), calls=%async_computation.3 | async-start | bytes 4194304 | tf_op jit(solution)/shard_map/psum | solution.py:51
  18.9 2.1 copy-start.1
  21.0 3.6 copy-start.7
  26.9 3.6 copy-start.9
  34.0 1.4 copy-start.8
  90.4 210.8 %all-reduce.9.cloned.1.call-start = ((), (), s32[]{:S(2)}) async-start(), calls=%async_computation.2 | async-start | bytes 7864320 | tf_op jit(solution)/shard_map/psum | solution.py:89
  185.8 2.1 copy-start.2
  185.8 2.1 copy-start.3
  189.3 236.2 %all-reduce.7.cloned.1.call-start = ((), (), s32[]{:S(2)}) async-start(), calls=%async_computation.1 | async-start | bytes 7864320 | tf_op jit(solution)/shard_map/psum | solution.py:89
  301.2 1.1 copy-start.4
  425.6 3.6 copy-start.5
Sparse Core Ops, SparseCore 0:
  17.5 66.9 all-gather.2
  90.5 73.3 all-reduce.10
  189.5 111.6 all-reduce.8
  303.5 122.0 all-reduce.6
